TPU v7x, 512 devices: a whole 4x8x8 slice. The times are simulated.
512 devices in a mesh: stn: 64 (over x, z_hi, y), tm: 8 (over z_lo, core).
Axes of the slice: x: 4, y: 8, z: 8 (z_hi: 2, z_lo: 4; z = z_hi * 4 + z_lo), core: 2. Of those that a mesh axis runs over, the one named last changes fastest.
Arguments:
- samples: bfloat16 [256, 32768], P('stn', 'tm'), may hold values from -200 to 200
- array_sizes: int32 [64], replicated, may hold values from 1 to 4, as said below
- partner: int32 [64], replicated, may hold values from 0 to 63, as said below
Outputs:
- correlation: float32 [1024, 4096], P(('stn', 'tm'))
- residual: float32 [1024, 4096], P(('stn', 'tm'))
Inputs may be any that keep to these rules, and one draw needn't show every extreme that they name: partner[i] = i XOR r for one round number r, 1 <= r < 64, the same for every i. Block i's live stations are its first array_sizes[i] slots.
All inputs are finite; a program needn't handle non-finite values.
Results may differ from a plain program's by a relative error of at most 0.0003.
Values may be sent and summed in bfloat16 or wider, within the bound.
A program may use at most 64 MiB of HBM per device.

v0:
```python
import math

import jax
import jax.numpy as jnp
from jax import lax
from jax.sharding import PartitionSpec as P

LAGS = 4096
DFT_P = 64
DFT_Q = 128


small_term = 1e-06
highest = lax.Precision.HIGHEST


def passed_along(value, axis, steps):
    count = lax.axis_size(axis)
    initial, last = (max(0, -steps), min(count, count - steps))
    return lax.ppermute(value, axis, [(source, source + steps) for source in range(initial, last)])


def swapped(shard, axis, stride):
    return lax.ppermute(shard, axis, [(i, i ^ 1 << stride) for i in range(lax.axis_size(axis))])


def phase_table(count_in, count_out, period):
    left = jnp.arange(count_in, dtype=jnp.int32)[:, None]
    right = jnp.arange(count_out, dtype=jnp.int32)[None, :]
    phase = (left * right % period).astype(jnp.float32) * (2.0 * math.pi / period)
    return (jnp.cos(phase), jnp.sin(phase))


def forward(windows):
    count = windows.shape[0]
    period = DFT_P * DFT_Q
    shaped = windows.reshape(count, DFT_P, DFT_Q)
    cos_first, sin_first = phase_table(DFT_P, DFT_P, DFT_P)
    first_re = jnp.einsum("rnq,nf->rfq", shaped, cos_first, precision=highest)
    first_im = -jnp.einsum("rnq,nf->rfq", shaped, sin_first, precision=highest)
    cos_twist, sin_twist = phase_table(DFT_P, DFT_Q, period)
    twist_re = first_re * cos_twist + first_im * sin_twist
    twist_im = first_im * cos_twist - first_re * sin_twist
    cos_second, sin_second = phase_table(DFT_Q, DFT_Q, DFT_Q)
    out_re = jnp.einsum("rfq,qg->rgf", twist_re, cos_second, precision=highest) + jnp.einsum(
        "rfq,qg->rgf", twist_im, sin_second, precision=highest
    )
    out_im = jnp.einsum("rfq,qg->rgf", twist_im, cos_second, precision=highest) - jnp.einsum(
        "rfq,qg->rgf", twist_re, sin_second, precision=highest
    )
    return (out_re.reshape(count, period), out_im.reshape(count, period))


def inverse(spec_re, spec_im):
    count = spec_re.shape[0]
    period = DFT_P * DFT_Q
    grid_re = spec_re.reshape(count, DFT_Q, DFT_P)
    grid_im = spec_im.reshape(count, DFT_Q, DFT_P)
    cos_first, sin_first = phase_table(DFT_Q, DFT_Q, DFT_Q)
    half_re = jnp.einsum("rgf,gk->rkf", grid_re, cos_first, precision=highest) - jnp.einsum(
        "rgf,gk->rkf", grid_im, sin_first, precision=highest
    )
    half_im = jnp.einsum("rgf,gk->rkf", grid_im, cos_first, precision=highest) + jnp.einsum(
        "rgf,gk->rkf", grid_re, sin_first, precision=highest
    )
    cos_twist, sin_twist = phase_table(DFT_Q, DFT_P, period)
    twist_re = half_re * cos_twist - half_im * sin_twist
    twist_im = half_im * cos_twist + half_re * sin_twist
    cos_last, sin_last = phase_table(DFT_P, DFT_P // 2, DFT_P)
    lagged = jnp.einsum("rkf,fj->rjk", twist_re, cos_last, precision=highest) - jnp.einsum(
        "rkf,fj->rjk", twist_im, sin_last, precision=highest
    )
    return lagged.reshape(count, LAGS)


def spectra(extended):
    count = extended.shape[0]
    blocks_here = extended.shape[1] // LAGS - 1
    values = extended.astype(jnp.float32).reshape(count, blocks_here + 1, LAGS)
    windows = jnp.concatenate([values[:, :-1], values[:, 1:]], axis=2).reshape(
        count * blocks_here, 2 * LAGS
    )
    spec_re, spec_im = forward(windows)
    spec_re = spec_re.reshape(count, blocks_here, 2 * LAGS)
    spec_im = spec_im.reshape(count, blocks_here, 2 * LAGS)
    partial_power = jnp.sum(spec_re * spec_re + spec_im * spec_im, axis=1)
    return (spec_re, spec_im, partial_power)


def whiten(spec_re, spec_im, power, total_windows):
    smooth = power
    for shift_by in (-2, -1, 1, 2):
        smooth = smooth + jnp.roll(power, shift_by, axis=1)
    level = smooth / 5.0 / total_windows + small_term
    inverse_root = 1.0 / jnp.sqrt(level)
    return (spec_re * inverse_root[:, None, :], spec_im * inverse_root[:, None, :], power / level)


def bit_set(round_number, bit):
    return jnp.bitwise_and(jnp.right_shift(round_number, bit), 1) == 1


def per_device(samples, array_sizes, partner):
    count = samples.shape[0]
    time_groups = lax.axis_size("tm")
    total_windows = samples.shape[1] // LAGS * time_groups
    block_id = lax.axis_index("stn")
    round_number = partner[0]
    other_id = jnp.bitwise_xor(block_id, round_number)
    block_ids = jnp.arange(array_sizes.shape[0], dtype=jnp.int32)
    live_own = jnp.sum(jnp.where(block_ids == block_id, array_sizes, 0))
    live_other = jnp.sum(jnp.where(block_ids == other_id, array_sizes, 0))
    rim = passed_along(samples, "tm", -1)
    extended = jnp.concatenate([samples, rim], axis=1)
    own_re, own_im, own_part = spectra(extended)
    own_power = lax.psum(own_part, "tm")
    own_re, own_im, own_auto = whiten(own_re, own_im, own_power, total_windows)
    bit_count = lax.axis_size("stn").bit_length() - 1
    moving = extended
    for bit in range(bit_count):

        def send_rows(held, bit=bit):
            return swapped(held, "stn", bit)

        def keep_rows_held(held):
            return held

        moving = lax.cond(bit_set(round_number, bit), send_rows, keep_rows_held, moving)
    far_re, far_im, far_part = spectra(moving)
    far_power = lax.psum(far_part, "tm")
    whitened_far = whiten(far_re, far_im, far_power, total_windows)
    far_re, far_im = (whitened_far[0], whitened_far[1])
    pair_count = count * count
    cross_re = (
        jnp.einsum("ajf,bjf->abf", own_re, far_re, precision=highest)
        + jnp.einsum("ajf,bjf->abf", own_im, far_im, precision=highest)
    ).reshape(pair_count, 2 * LAGS)
    cross_im = (
        jnp.einsum("ajf,bjf->abf", own_re, far_im, precision=highest)
        - jnp.einsum("ajf,bjf->abf", own_im, far_re, precision=highest)
    ).reshape(pair_count, 2 * LAGS)
    ratio = own_auto / (jnp.mean(own_auto, axis=1, keepdims=True) + small_term)
    keep_rows = jnp.repeat(1.0 - ratio, count, axis=0)
    pair_ids = jnp.arange(pair_count, dtype=jnp.int32)
    live = ((pair_ids // count < live_own) & (pair_ids % count < live_other)).astype(jnp.float32)
    norm_factor = 1.0 / math.sqrt(2 * LAGS * total_windows)
    share = pair_count // time_groups
    first_row = lax.axis_index("tm") * share
    plain_lags = inverse(cross_re, cross_im)
    refined_lags = inverse(cross_re * keep_rows, cross_im * keep_rows)
    summed = lax.psum_scatter(
        jnp.concatenate([plain_lags, refined_lags], axis=1) * norm_factor,
        "tm",
        scatter_dimension=0,
        tiled=True,
    )
    correlation = summed[:, :LAGS]
    residual = summed[:, LAGS:]
    share_live = lax.dynamic_slice_in_dim(live, first_row, share, 0)[:, None]
    return (correlation * share_live, residual * share_live)


def solution(mesh):
    placed = (P("stn", "tm"), P(), P())
    return jax.shard_map(
        per_device,
        mesh=mesh,
        in_specs=placed,
        out_specs=(P(("stn", "tm"), None), P(("stn", "tm"), None)),
        check_vma=False,
    )
```

profile of v0, /device:TPU:1, one launch (start us, length us, event | category | flops | bytes accessed | tf_op | source)
XLA Modules:
  0.0 252.2 jit_solution(7621787634445726067)
XLA Ops:
  7.2 8.8 %collective-permute-start.6 = (bf16[4,4096]{1,0:T(4,128)(2,1)}, bf16[4,4096]{1,0:T(4,128)(2,1)S(1)}, u32[]{:S(2)}, u32[]{:S(2)}) collective-permute-start(bf16[4,4096]{1,0:T(4,128)(2,1)} %param.15), channel_id=1, source_target_pairs={{1,0},{2,1},{3,2},{4,3},{5,4},{6,5},{7,6},{9,8},{10,9},{11,10},{12... | collective-permute-start | bytes 98312 | tf_op jit(solution)/shard_map/ppermute | solution.py:20
  19.1 5.1 %conditional.6 = (bf16[4,8192]{1,0:T(4,128)(2,1)S(1)}) conditional(s32[]{:T(128)} %convert_element_type.140, bf16[4,8192]{1,0:T(4,128)(2,1)S(1)} %pad_maximum_fusion, bf16[4,8192]{1,0:T(4,128)(2,1)S(1)} %pad_maximum_fusion), branch_computations={%region_0.1_spmd, %region_1.2_spmd} | conditional | bytes 393264 | solution.py:128
  19.1 1.9 collective-permute-start
  21.0 3.1 %collective-permute-done = bf16[4,8192]{1,0:T(4,128)(2,1)S(1)} collective-permute-done((bf16[4,8192]{1,0:T(4,128)(2,1)S(1)}, bf16[4,8192]{1,0:T(4,128)(2,1)S(1)}, u32[]{:S(2)}, u32[]{:S(2)}) %collective-permute-start) | collective-permute-done | bytes 65568 | tf_op jit(solution)/shard_map/cond/branch_1_fun/ppermute | solution.py:24
  24.1 6.7 %conditional.7 = (bf16[4,8192]{1,0:T(4,128)(2,1)S(1)}) conditional(s32[]{:T(128)} %convert_element_type.139, bf16[4,8192]{1,0:T(4,128)(2,1)S(1)} %get-tuple-element.75, bf16[4,8192]{1,0:T(4,128)(2,1)S(1)} %get-tuple-element.75), branch_computations={%region_2.3_spmd, %region_3.4_spmd} | conditional | bytes 393264 | solution.py:128
  24.2 1.9 collective-permute-start.1
  26.1 4.7 %collective-permute-done.1 = bf16[4,8192]{1,0:T(4,128)(2,1)S(1)} collective-permute-done((bf16[4,8192]{1,0:T(4,128)(2,1)S(1)}, bf16[4,8192]{1,0:T(4,128)(2,1)S(1)}, u32[]{:S(2)}, u32[]{:S(2)}) %collective-permute-start.1) | collective-permute-done | bytes 65568 | tf_op jit(solution)/shard_map/cond/branch_1_fun/ppermute | solution.py:24
  30.8 9.0 %conditional.8 = (bf16[4,8192]{1,0:T(4,128)(2,1)S(1)}) conditional(s32[]{:T(128)} %convert_element_type.138, bf16[4,8192]{1,0:T(4,128)(2,1)S(1)} %get-tuple-element.76, bf16[4,8192]{1,0:T(4,128)(2,1)S(1)} %get-tuple-element.76), branch_computations={%region_4.5_spmd, %region_5.6_spmd} | conditional | bytes 393264 | solution.py:128
  30.8 5.5 %collective-permute-start.2 = (bf16[4,8192]{1,0:T(4,128)(2,1)S(1)}, bf16[4,8192]{1,0:T(4,128)(2,1)S(1)}, u32[]{:S(2)}, u32[]{:S(2)}) collective-permute-start(bf16[4,8192]{1,0:T(4,128)(2,1)S(1)} %param.5), channel_id=1, source_target_pairs={{0,32},{8,40},{16,48},{24,56},{32,0},{40,8},{48,16},{56,24},{64,96... | collective-permute-start | bytes 196616 | tf_op jit(solution)/shard_map/cond/branch_1_fun/ppermute | solution.py:24
  36.3 3.4 %collective-permute-done.2 = bf16[4,8192]{1,0:T(4,128)(2,1)S(1)} collective-permute-done((bf16[4,8192]{1,0:T(4,128)(2,1)S(1)}, bf16[4,8192]{1,0:T(4,128)(2,1)S(1)}, u32[]{:S(2)}, u32[]{:S(2)}) %collective-permute-start.2) | collective-permute-done | bytes 65568 | tf_op jit(solution)/shard_map/cond/branch_1_fun/ppermute | solution.py:24
  39.8 10.6 %conditional.9 = (bf16[4,8192]{1,0:T(4,128)(2,1)S(1)}) conditional(s32[]{:T(128)} %convert_element_type.137, bf16[4,8192]{1,0:T(4,128)(2,1)S(1)} %get-tuple-element.77, bf16[4,8192]{1,0:T(4,128)(2,1)S(1)} %get-tuple-element.77), branch_computations={%region_6.7_spmd, %region_7.8_spmd} | conditional | bytes 393264 | solution.py:128
  39.8 8.9 %collective-permute-start.3 = (bf16[4,8192]{1,0:T(4,128)(2,1)S(1)}, bf16[4,8192]{1,0:T(4,128)(2,1)S(1)}, u32[]{:S(2)}, u32[]{:S(2)}) collective-permute-start(bf16[4,8192]{1,0:T(4,128)(2,1)S(1)} %param.7), channel_id=1, source_target_pairs={{0,64},{8,72},{16,80},{24,88},{32,96},{40,104},{48,112},{56,120},{... | collective-permute-start | bytes 196616 | tf_op jit(solution)/shard_map/cond/branch_1_fun/ppermute | solution.py:24
  48.7 1.7 collective-permute-done.3
  50.5 5.1 %conditional.10 = (bf16[4,8192]{1,0:T(4,128)(2,1)S(1)}) conditional(s32[]{:T(128)} %convert_element_type.136, bf16[4,8192]{1,0:T(4,128)(2,1)S(1)} %get-tuple-element.78, bf16[4,8192]{1,0:T(4,128)(2,1)S(1)} %get-tuple-element.78), branch_computations={%region_8.9_spmd, %region_9.10_spmd} | conditional | bytes 393264 | solution.py:128
  50.5 3.1 %collective-permute-start.4 = (bf16[4,8192]{1,0:T(4,128)(2,1)S(1)}, bf16[4,8192]{1,0:T(4,128)(2,1)S(1)}, u32[]{:S(2)}, u32[]{:S(2)}) collective-permute-start(bf16[4,8192]{1,0:T(4,128)(2,1)S(1)} %param.9), channel_id=1, source_target_pairs={{0,128},{8,136},{16,144},{24,152},{32,160},{40,168},{48,176},{56,1... | collective-permute-start | bytes 196616 | tf_op jit(solution)/shard_map/cond/branch_1_fun/ppermute | solution.py:24
  53.6 1.9 collective-permute-done.4
  59.1 0.5 fusion.2
  59.9 0.5 fusion.3
  60.7 0.7 multiply_add_fusion
  61.4 0.7 multiply_add_fusion.2
  62.5 79.2 %all-reduce.7.cloned.1.call-done = (f32[4,8192]{1,0:T(4,128)}, f32[4,8192]{1,0:T(4,128)}) async-done(((f32[4,8192]{1,0:T(4,128)}, f32[4,8192]{1,0:T(4,128)}), (f32[4,8192]{1,0:T(4,128)}, f32[4,8192]{1,0:T(4,128)})) %all-reduce.7.cloned.1.call-update) | async-done | bytes 262160 | tf_op jit(solution)/shard_map/psum | solution.py:116
  141.7 1.2 fusion.265
  143.2 0.7 copy-done.4
  145.3 0.5 reshape_reshape.30
  145.9 1.5 reshape.156
  147.4 0.5 reshape_reshape.31
  147.9 2.7 %fusion.260 = (f32[16,128,64]{2,1,0:T(8,128)}, f32[16,128,64]{2,1,0:T(8,128)}) fusion(f32[16,128,64]{2,1,0:T(8,128)S(1)} %reshape_reshape.30, f32[16,128,64]{2,1,0:T(8,128)} %reshape.156, f32[16,128,64]{2,1,0:T(8,128)S(1)} %reshape_reshape.31), kind=kLoop, calls=%fused_computation.291 | loop fusion | flops 262144 | bytes 2621440 | tf_op jit(solution)/shard_map/mul | solution.py:150
  150.7 1.5 copy.35
  152.2 0.8 fusion.128
  153.0 1.6 fusion.114
  154.7 1.5 copy.36
  156.2 1.6 fusion.116
  157.8 1.6 fusion.126
  160.1 0.8 fusion.124
  160.9 0.8 fusion.110
  161.8 0.8 fusion.112
  162.6 0.8 fusion.122
  163.9 0.5 fusion.5
  164.4 0.5 convolution_subtract_fusion
  165.1 0.5 fusion.8
  165.7 0.5 convolution_subtract_fusion.1
  166.4 0.8 maximum_multiply_fusion
  167.3 1.3 dynamic-slice
  169.2 0.6 copy-done.6
  169.9 0.6 fusion.160
  170.5 1.3 and_convert_fusion
  171.9 71.8 %all-reduce.5.cloned.1.call-done = f32[16,8192]{1,0:T(8,128)} async-done(((f32[16,8192]{1,0:T(8,128)}), f32[16,8192]{1,0:T(8,128)}) %all-reduce.5.cloned.1.call-update) | async-done | bytes 524304
  243.7 1.7 dynamic-slice_multiply_fusion
  (70 shorter events, 10.5 us)
Async XLA Ops:
  7.2 134.5 %all-reduce.7.cloned.1.call-start = ((), (), s32[]{:S(2)}) async-start(), calls=%async_computation.1 | async-start | bytes 524288 | tf_op jit(solution)/shard_map/psum | solution.py:116
  7.2 9.8 %collective-permute-start.6 = (bf16[4,4096]{1,0:T(4,128)(2,1)}, bf16[4,4096]{1,0:T(4,128)(2,1)S(1)}, u32[]{:S(2)}, u32[]{:S(2)}) collective-permute-start(bf16[4,4096]{1,0:T(4,128)(2,1)} %param.15), channel_id=1, source_target_pairs={{1,0},{2,1},{3,2},{4,3},{5,4},{6,5},{7,6},{9,8},{10,9},{11,10},{12... | collective-permute-start | bytes 98312 | tf_op jit(solution)/shard_map/ppermute | solution.py:20
  16.0 0.7 copy-start.7
  16.2 0.9 copy-start.5
  19.1 5.0 %collective-permute-start = (bf16[4,8192]{1,0:T(4,128)(2,1)S(1)}, bf16[4,8192]{1,0:T(4,128)(2,1)S(1)}, u32[]{:S(2)}, u32[]{:S(2)}) collective-permute-start(bf16[4,8192]{1,0:T(4,128)(2,1)S(1)} %param.1), channel_id=1, source_target_pairs={{0,8},{8,0},{16,24},{24,16},{32,40},{40,32},{48,56},{56,48},{64,72... | collective-permute-start | bytes 196616 | tf_op jit(solution)/shard_map/cond/branch_1_fun/ppermute | solution.py:24
  24.2 6.6 %collective-permute-start.1 = (bf16[4,8192]{1,0:T(4,128)(2,1)S(1)}, bf16[4,8192]{1,0:T(4,128)(2,1)S(1)}, u32[]{:S(2)}, u32[]{:S(2)}) collective-permute-start(bf16[4,8192]{1,0:T(4,128)(2,1)S(1)} %param.3), channel_id=1, source_target_pairs={{0,16},{8,24},{16,0},{24,8},{32,48},{40,56},{48,32},{56,40},{64,80... | collective-permute-start | bytes 196616 | tf_op jit(solution)/shard_map/cond/branch_1_fun/ppermute | solution.py:24
  30.8 9.0 %collective-permute-start.2 = (bf16[4,8192]{1,0:T(4,128)(2,1)S(1)}, bf16[4,8192]{1,0:T(4,128)(2,1)S(1)}, u32[]{:S(2)}, u32[]{:S(2)}) collective-permute-start(bf16[4,8192]{1,0:T(4,128)(2,1)S(1)} %param.5), channel_id=1, source_target_pairs={{0,32},{8,40},{16,48},{24,56},{32,0},{40,8},{48,16},{56,24},{64,96... | collective-permute-start | bytes 196616 | tf_op jit(solution)/shard_map/cond/branch_1_fun/ppermute | solution.py:24
  39.8 10.6 %collective-permute-start.3 = (bf16[4,8192]{1,0:T(4,128)(2,1)S(1)}, bf16[4,8192]{1,0:T(4,128)(2,1)S(1)}, u32[]{:S(2)}, u32[]{:S(2)}) collective-permute-start(bf16[4,8192]{1,0:T(4,128)(2,1)S(1)} %param.7), channel_id=1, source_target_pairs={{0,64},{8,72},{16,80},{24,88},{32,96},{40,104},{48,112},{56,120},{... | collective-permute-start | bytes 196616 | tf_op jit(solution)/shard_map/cond/branch_1_fun/ppermute | solution.py:24
  50.5 5.0 %collective-permute-start.4 = (bf16[4,8192]{1,0:T(4,128)(2,1)S(1)}, bf16[4,8192]{1,0:T(4,128)(2,1)S(1)}, u32[]{:S(2)}, u32[]{:S(2)}) collective-permute-start(bf16[4,8192]{1,0:T(4,128)(2,1)S(1)} %param.9), channel_id=1, source_target_pairs={{0,128},{8,136},{16,144},{24,152},{32,160},{40,168},{48,176},{56,1... | collective-permute-start | bytes 196616 | tf_op jit(solution)/shard_map/cond/branch_1_fun/ppermute | solution.py:24
  62.1 181.6 %all-reduce.5.cloned.1.call-start = ((), (), s32[]{:S(2)}) async-start(), calls=%async_computation | async-start | bytes 1048576
  141.7 1.2 copy-start
  143.0 0.9 copy-start.4
  161.8 1.7 copy-start.3
  162.6 1.1 copy-start.1
  162.6 1.2 copy-start.2
  169.2 0.7 copy-start.6
Sparse Core Ops, SparseCore 0:
  62.2 79.4 all-reduce.6
  167.4 76.3 all-reduce.4
where the time goes:
time: 254 us; the launch traced here: 252 us
  waiting for transfers between devices  166 us (65%)
  starting transfers between devices  30.4 us (12%)
  matrix products  16.9 us (7%)
  between operations  15.4 us (6%)
  local copies, waits for them, and re-layouts  13.3 us (5%)
  other arithmetic  9.95 us (4%)
    psum x1, waiting for transfers between devices, per_device(): own_power = lax.psum(own_part, 'tm')  79.2 us
    unnamed x3, waiting for transfers between devices  71.9 us
    ppermute x5, starting transfers between devices, swapped(): lax.ppermute(shard, axis, [(i, i ^ 1 << stride) for i in range(lax.axis_s...  21.4 us
    ppermute x5, waiting for transfers between devices, swapped(): lax.ppermute(shard, axis, [(i, i ^ 1 << stride) for i in range(lax.axis_s...  14.8 us
    unnamed x8, matrix products  9 us
    ppermute x1, starting transfers between devices, passed_along(): lax.ppermute(value, axis, [(source, source + steps) for source in range(i...  8.79 us
  transfers between devices with their start and end apart: 8, of which 8 were waited for; matrix products, arithmetic and copies ran while one was open for 1% of the time, Pallas kernels for 0%

commit v1 on v0

v1 whole, which is shorter than its diff:
```python
import math

import jax
import jax.numpy as jnp
import ml_dtypes
import numpy as np
from jax import lax
from jax.experimental import pallas as pl
from jax.experimental.pallas import tpu as pltpu
from jax.sharding import PartitionSpec as P

LAGS = 4096
SPECTRUM = 8192
WINDOWS = 8
STN_DEV = 4
LINE = 8
LANES = 128
COARSE = 64
HALO = 2
ROWS = 40
N1_BLOCK = LAGS // LANES
REC_ROWS = (WINDOWS + 1) * N1_BLOCK
SMALL = 1e-06
F32 = jnp.float32
BF16 = jnp.bfloat16


def split_table(table):
    high = table.astype(ml_dtypes.bfloat16)
    low = (table - high.astype(np.float64)).astype(ml_dtypes.bfloat16)
    return high, low


def tables():
    f1 = np.arange(ROWS) - HALO
    n1 = np.arange(COARSE)
    n2 = np.arange(LANES)
    phase = 2.0 * np.pi * (np.outer(f1, n1) % COARSE) / COARSE
    first = np.concatenate([np.cos(phase), -np.sin(phase)], axis=0)
    first = np.concatenate(split_table(first), axis=1)
    phase = 2.0 * np.pi * np.outer(f1, n2) / SPECTRUM
    twist = np.concatenate([np.cos(phase), np.sin(phase)], axis=1).astype(np.float32)
    phase = 2.0 * np.pi * (np.outer(n2, n2) % LANES) / LANES
    cos, sin = np.cos(phase), np.sin(phase)
    second = np.block([[cos, -sin], [sin, cos]])
    second = np.concatenate(split_table(second), axis=1)
    weight = np.where((f1 == 0) | (f1 == COARSE // 2), 1.0, 2.0) * ((f1 >= 0) & (f1 <= COARSE // 2))
    lag1 = np.arange(N1_BLOCK)
    phase = 2.0 * np.pi * (np.outer(lag1, f1) % COARSE) / COARSE
    scale = 1.0 / math.sqrt(SPECTRUM * WINDOWS)
    last = np.concatenate([np.cos(phase) * weight, np.sin(phase) * weight], axis=1) * scale
    high, low = split_table(last)
    last = np.concatenate([high, low, high], axis=1)
    share = np.broadcast_to((weight / SPECTRUM)[:, None], (ROWS, LANES)).astype(np.float32)
    return first, twist, second, last, share


def halves(value):
    high = value.astype(BF16)
    low = (value - high.astype(F32)).astype(BF16)
    return high, low


def twisted(re, im, cos, sin):
    return re * cos + im * sin, im * cos - re * sin


def gather_kernel(own_ref, far_ref, out_ref, local_sem, send_sem, recv_sem):
    stn = lax.axis_index("stn")
    me = lax.axis_index("tm")
    barrier = pltpu.get_barrier_semaphore()
    for d in range(1, LINE):
        peer = lax.rem(me + d, LINE)
        pl.semaphore_signal(barrier, inc=1, device_id=(stn, peer), device_id_type=pl.DeviceIdType.MESH)
    my_rows = pl.ds(pl.multiple_of(me * N1_BLOCK, N1_BLOCK), N1_BLOCK)
    local = [
        pltpu.make_async_copy(own_ref.at[pl.ds(me // 2, 1)], out_ref.at[pl.ds(0, 1), my_rows], local_sem.at[0]),
        pltpu.make_async_copy(
            far_ref.at[pl.ds(lax.rem(me, 2) * 2, 2)], out_ref.at[pl.ds(1, 2), my_rows], local_sem.at[1]
        ),
    ]
    for copy in local:
        copy.start()
    out_ref[:, WINDOWS * N1_BLOCK :, :] = jnp.zeros((3, N1_BLOCK, LANES), BF16)
    pl.semaphore_wait(barrier, LINE - 1)
    copies = []
    for d in range(1, LINE):
        peer = lax.rem(me + d, LINE)
        for kind in (1, 0):
            if kind:
                src = far_ref.at[pl.ds(lax.rem(peer, 2) * 2, 2)]
                dst = out_ref.at[pl.ds(1, 2), my_rows]
            else:
                src = own_ref.at[pl.ds(peer // 2, 1)]
                dst = out_ref.at[pl.ds(0, 1), my_rows]
            copy = pltpu.make_async_remote_copy(
                src_ref=src,
                dst_ref=dst,
                send_sem=send_sem.at[kind, d],
                recv_sem=recv_sem.at[kind, d],
                device_id=(stn, peer),
                device_id_type=pl.DeviceIdType.MESH,
            )
            copy.start()
            copies.append(copy)
    for copy in local:
        copy.wait()
    for copy in copies:
        copy.wait()


def gather_line(own, far):
    return pl.pallas_call(
        gather_kernel,
        name="gather_line",
        out_shape=jax.ShapeDtypeStruct((3, REC_ROWS, LANES), BF16),
        in_specs=[pl.BlockSpec(memory_space=pltpu.VMEM)] * 2,
        out_specs=pl.BlockSpec(memory_space=pltpu.VMEM),
        scratch_shapes=[
            pltpu.SemaphoreType.DMA((2,)),
            pltpu.SemaphoreType.DMA((2, LINE)),
            pltpu.SemaphoreType.DMA((2, LINE)),
        ],
        compiler_params=pltpu.CompilerParams(collective_id=0, has_side_effects=True),
    )(own, far)


def correlate_kernel(
    sizes_ref, partner_ref, place_ref, rec_ref, first_ref, twist_ref, second_ref, last_ref, share_ref,
    plain_ref, refined_ref, left_ref, spec_ref,
):
    cos, sin = twist_ref[:, :LANES], twist_ref[:, LANES:]
    cos2, sin2 = jnp.concatenate([cos, cos], axis=0), jnp.concatenate([sin, sin], axis=0)
    first = first_ref[...]
    second_hi, second_lo = second_ref[:, : 2 * LANES], second_ref[:, 2 * LANES :]
    roots = []
    powers = []
    levels = []
    for s in range(3):
        for j in range(0, WINDOWS, 2):
            one = rec_ref[s, j * N1_BLOCK : (j + 2) * N1_BLOCK, :]
            two = rec_ref[s, (j + 1) * N1_BLOCK : (j + 3) * N1_BLOCK, :]
            both = jnp.concatenate([one, two], axis=1)
            grid = jnp.dot(first, jnp.concatenate([both, both], axis=0), preferred_element_type=F32)
            re = jnp.concatenate([grid[:ROWS, :LANES], grid[:ROWS, LANES:]], axis=0)
            im = jnp.concatenate([grid[ROWS:, :LANES], grid[ROWS:, LANES:]], axis=0)
            re, im = twisted(re, im, cos2, sin2)
            rows = slice((s * WINDOWS + j) * ROWS, (s * WINDOWS + j + 2) * ROWS)
            re_hi, re_lo = halves(re)
            im_hi, im_lo = halves(im)
            left_ref[rows, :] = jnp.concatenate([re_hi, im_hi, re_lo, im_lo], axis=1)
        rows = slice(s * WINDOWS * ROWS, (s + 1) * WINDOWS * ROWS)
        left_hi = left_ref[rows, : 2 * LANES]
        left_lo = left_ref[rows, 2 * LANES :]
        spec_ref[rows, :] = (
            jnp.dot(left_hi, second_hi, preferred_element_type=F32)
            + jnp.dot(left_lo, second_hi, preferred_element_type=F32)
            + jnp.dot(left_hi, second_lo, preferred_element_type=F32)
        )
        power = jnp.zeros((ROWS, LANES), F32)
        for j in range(WINDOWS):
            one = spec_ref[(s * WINDOWS + j) * ROWS : (s * WINDOWS + j + 1) * ROWS, :]
            one = one * one
            power = power + one[:, :LANES] + one[:, LANES:]
        smooth = power
        for shift in (-2, -1, 1, 2):
            smooth = smooth + pltpu.roll(power, shift % ROWS, axis=0)
        level = smooth / 5.0 / WINDOWS + SMALL
        roots.append(1.0 / jnp.sqrt(level))
        powers.append(power)
        levels.append(level)

    auto = powers[0] / levels[0]
    mean = jnp.sum(auto * share_ref[...])
    keep = 1.0 - auto / (mean + SMALL)

    cross = []
    sums = [[jnp.zeros((ROWS, LANES), F32) for _ in range(2)] for _ in range(2)]
    for j in range(WINDOWS):
        source = spec_ref[j * ROWS : (j + 1) * ROWS, :]
        a_re, a_im = source[:, :LANES] * roots[0], source[:, LANES:] * roots[0]
        for b in range(2):
            start = ((b + 1) * WINDOWS + j) * ROWS
            target = spec_ref[start : start + ROWS, :]
            b_re, b_im = target[:, :LANES] * roots[b + 1], target[:, LANES:] * roots[b + 1]
            sums[b][0] = sums[b][0] + (a_re * b_re + a_im * b_im)
            sums[b][1] = sums[b][1] + (a_im * b_re - a_re * b_im)
    for b in range(2):
        plain = jnp.concatenate(sums[b], axis=1)
        cross.append(plain)
        cross.append(plain * jnp.concatenate([keep, keep], axis=1))
    cross = jnp.concatenate(cross, axis=0)
    cross_hi, cross_lo = halves(cross)
    half = (
        jnp.dot(cross_hi, second_hi, preferred_element_type=F32)
        + jnp.dot(cross_lo, second_hi, preferred_element_type=F32)
        + jnp.dot(cross_hi, second_lo, preferred_element_type=F32)
    )
    columns = []
    for i in range(4):
        part = half[i * ROWS : (i + 1) * ROWS]
        re, im = twisted(part[:, :LANES], part[:, LANES:], cos, sin)
        columns.append(jnp.concatenate([re, im], axis=0))
    columns = jnp.concatenate(columns, axis=1)
    col_hi, col_lo = halves(columns)
    lags = jnp.dot(last_ref[...], jnp.concatenate([col_hi, col_hi, col_lo], axis=0), preferred_element_type=F32)

    block = place_ref[0]
    line = place_ref[1]
    source_live = (line // 2 < sizes_ref[block]).astype(F32)
    other_size = sizes_ref[partner_ref[block]]
    for b in range(2):
        live = source_live * (lax.rem(line, 2) * 2 + b < other_size).astype(F32)
        for kind, ref in enumerate((plain_ref, refined_ref)):
            index = 2 * b + kind
            value = lags[:, index * LANES : (index + 1) * LANES] * live
            for k in range(N1_BLOCK):
                ref[b : b + 1, k * LANES : (k + 1) * LANES] = value[k : k + 1, :]


def correlate(array_sizes, partner, place, record):
    out = jax.ShapeDtypeStruct((2, LAGS), F32)
    smem = pl.BlockSpec(memory_space=pltpu.SMEM)
    vmem = pl.BlockSpec(memory_space=pltpu.VMEM)
    return pl.pallas_call(
        correlate_kernel,
        name="correlate",
        out_shape=(out, out),
        in_specs=[smem] * 3 + [vmem] * 6,
        out_specs=(vmem, vmem),
        scratch_shapes=[
            pltpu.VMEM((3 * WINDOWS * ROWS, 4 * LANES), BF16),
            pltpu.VMEM((3 * WINDOWS * ROWS, 2 * LANES), F32),
        ],
    )(array_sizes, partner, place, record, *(jnp.asarray(table) for table in tables()))


def per_device(samples, array_sizes, partner):
    count = lax.axis_size("stn")
    own = samples.reshape(STN_DEV, N1_BLOCK, LANES)

    def moved(round_number):
        return lambda rows: lax.ppermute(rows, "stn", [(i, i ^ round_number) for i in range(count)])

    far = lax.switch(partner[0] - 1, [moved(r) for r in range(1, count)], own)
    record = gather_line(own, far)
    place = jnp.stack([lax.axis_index("stn"), lax.axis_index("tm")]).astype(jnp.int32)
    return correlate(array_sizes, partner, place, record)


def solution(mesh):
    placed = (P("stn", "tm"), P(), P())
    return jax.shard_map(
        per_device,
        mesh=mesh,
        in_specs=placed,
        out_specs=(P(("stn", "tm"), None), P(("stn", "tm"), None)),
        check_vma=False,
    )
```

time: 254 us -> 60.1 us (0.24)
  waiting for transfers between devices: 166 us -> 13.2 us
  Pallas kernels: 0 us -> 24.3 us
  matrix products: 16.9 us -> 0 us
  between operations: 15.4 us -> 0.69 us
  local copies, waits for them, and re-layouts: 13.3 us -> 1.42 us
  starting transfers between devices: 30.4 us -> 19.5 us
  other arithmetic: 9.95 us -> 0.6 us
    psum x1 -> x0, waiting for transfers between devices: 79.2 us -> none  [per_device(): own_power = lax.psum(own_part, 'tm')]
    unnamed x3 -> x0, waiting for transfers between devices: 71.9 us -> none
    pallas_call x0 -> x2, Pallas kernels: none -> 24.3 us  [the longest x1 21.1 us: gather_line(): pl.pallas_call(gather_kernel, name='gather_line', out_shape=jax.ShapeDtyp...]
    ppermute x6 -> x1, starting transfers between devices: 30.2 us -> 19.5 us  [moved(): lax.ppermute(rows, 'stn', [(i, i ^ round_number) for i in range(count)])]
    unnamed x8 -> x0, matrix products: 9 us -> none
    dot_general x16 -> x0, matrix products: 7.95 us -> none  [the longest x2 1.08 us: inverse(): jnp.einsum('rkf,fj->rjk', twist_im, sin_last, precision=highest)]
    mul x5 -> x0, other arithmetic: 5.54 us -> none  [the longest x1 2.74 us: per_device(): refined_lags = inverse(cross_re * keep_rows, cross_im * keep_rows)]
    mul x2 -> x0, local copies, waits for them, and re-layouts: 3.07 us -> none  [per_device(): refined_lags = inverse(cross_re * keep_rows, cross_im * keep_rows)]
  transfers between devices with their start and end apart: 8 -> 1, of which waited for: 8 -> 1; matrix products, arithmetic and copies ran while one was open for 1% -> 0% of each run, Pallas kernels for 0% -> 0%
where the time goes in v1:
time: 60.1 us; the launch traced here: 59.8 us
  Pallas kernels  24.3 us (40%)
  starting transfers between devices  19.5 us (32%)
  waiting for transfers between devices  13.2 us (22%)
  local copies, waits for them, and re-layouts  1.42 us (2%)
  between operations  0.69 us (1%)
    pallas_call x1, Pallas kernels, gather_line(): pl.pallas_call(gather_kernel, name='gather_line', out_shape=jax.ShapeDtyp...  21.1 us
    ppermute x1, starting transfers between devices, moved(): lax.ppermute(rows, 'stn', [(i, i ^ round_number) for i in range(count)])  19.5 us
    ppermute x1, waiting for transfers between devices, moved(): lax.ppermute(rows, 'stn', [(i, i ^ round_number) for i in range(count)])  13.2 us
    pallas_call x1, Pallas kernels, correlate(): pl.pallas_call(correlate_kernel, name='correlate', out_shape=(out, out),...  3.21 us
    unnamed x3, local copies, waits for them, and re-layouts  1.42 us
  transfers between devices with their start and end apart: 1, of which 1 were waited for; matrix products, arithmetic and copies ran while one was open for 0% of the time, Pallas kernels for 0%

profile of v1, /device:TPU:1, one launch (start us, length us, event | category | flops | bytes accessed | tf_op | source)
XLA Modules:
  0.0 59.8 jit_solution(16853353547653343822)
XLA Ops:
  0.6 0.6 %pad_add_fusion.place_ref = s32[2]{0:T(128)} fusion(s32[1]{0:T(128)} %bitcast.1, s32[1]{0:T(128)} %bitcast), kind=kLoop, calls=%fused_computation.1 | loop fusion | flops 2 | bytes 16 | tf_op jit(solution)/shard_map/stack | solution.py:247
  1.2 0.0 copy-start
  1.2 0.7 %copy-done = s32[64]{0:T(128)S(1)} copy-done((s32[64]{0:T(128)S(1)}, s32[64]{0:T(128)}, u32[]{:S(2)}) %copy-start) | copy-done | bytes 280
  1.9 0.8 %copy.12 = bf16[1,4,32,128]{3,2,1,0:T(8,128)(2,1)S(1)} copy(bf16[1,4,32,128]{3,1,2,0:T(4,128)(2,1)} %bitcast.72) | data formatting | bytes 65536
  2.7 32.8 %conditional.1 = (bf16[4,32,128]{2,1,0:T(8,128)(2,1)}) conditional(s32[]{:T(128)} %bitcast.2, bf16[4,32,128]{2,1,0:T(8,128)(2,1)S(1)} %bitcast.39, bf16[4,32,128]{2,1,0:T(8,128)(2,1)S(1)} %bitcast.70, bf16[4,32,128]{2,1,0:T(8,128)(2,1)S(1)} %bitcast.10, bf16[4,32,128]{2,1,0:T(8,128)(2,1)S(1)} %bitcast.11, ...), branch_computations={%region_0.0_spmd, %region_1.0_spmd, %region_2.0_spmd, %region_3.0_... | conditional | bytes 131120 | solution.py:245
  2.7 19.5 %collective-permute-start.41 = (bf16[4,32,128]{2,1,0:T(8,128)(2,1)S(1)}, bf16[4,32,128]{2,1,0:T(8,128)(2,1)}, u32[]{:S(2)}, u32[]{:S(2)}) collective-permute-start(bf16[4,32,128]{2,1,0:T(8,128)(2,1)S(1)} %param.41), channel_id=1, source_target_pairs={{0,336},{8,344},{16,320},{24,328},{32,368},{40,376},{48,352},{56,3... | collective-permute-start | bytes 98312 | tf_op jit(solution)/shard_map/cond/branch_41_fun/ppermute | solution.py:243
  22.2 13.2 %collective-permute-done.41 = bf16[4,32,128]{2,1,0:T(8,128)(2,1)} collective-permute-done((bf16[4,32,128]{2,1,0:T(8,128)(2,1)S(1)}, bf16[4,32,128]{2,1,0:T(8,128)(2,1)}, u32[]{:S(2)}, u32[]{:S(2)}) %collective-permute-start.41) | collective-permute-done | bytes 32800 | tf_op jit(solution)/shard_map/cond/branch_41_fun/ppermute | solution.py:243
  35.5 21.1 %gather_line.1.rec_ref = bf16[3,288,128]{2,1,0:T(8,128)(2,1)} custom-call(bf16[4,32,128]{2,1,0:T(8,128)(2,1)S(1)} %bitcast.71, bf16[4,32,128]{2,1,0:T(8,128)(2,1)} %get-tuple-element.129.far_ref), custom_call_target="tpu_custom_call" | custom-call | tf_op jit(solution)/shard_map/gather_line/pallas_call | solution.py:113
  56.6 3.2 %correlate.1 = (f32[2,4096]{1,0:T(2,128)}, f32[2,4096]{1,0:T(2,128)}) custom-call(s32[64]{0:T(128)} %sizes_ref.1, s32[64]{0:T(128)} %partner_ref.1, s32[2]{0:T(128)} %pad_add_fusion.place_ref, bf16[3,288,128]{2,1,0:T(8,128)(2,1)} %gather_line.1.rec_ref, bf16[80,128]{1,0:T(8,128)(2,1)} %constant.29.clone.first_ref, f32[40,256]{1,0:T(8,128)} %constant.30.clone.twist_ref, ...), custom_call_target="tpu_custom_call" | custom-call | tf_op jit(solution)/shard_map/correlate/pallas_call | solution.py:225
Async XLA Ops:
  1.2 0.7 %copy-start = (s32[64]{0:T(128)S(1)}, s32[64]{0:T(128)}, u32[]{:S(2)}) copy-start(s32[64]{0:T(128)} %partner_ref.1) | copy-start | bytes 772
  2.7 32.8 %collective-permute-start.41 = (bf16[4,32,128]{2,1,0:T(8,128)(2,1)S(1)}, bf16[4,32,128]{2,1,0:T(8,128)(2,1)}, u32[]{:S(2)}, u32[]{:S(2)}) collective-permute-start(bf16[4,32,128]{2,1,0:T(8,128)(2,1)S(1)} %param.41), channel_id=1, source_target_pairs={{0,336},{8,344},{16,320},{24,328},{32,368},{40,376},{48,352},{56,3... | collective-permute-start | bytes 98312 | tf_op jit(solution)/shard_map/cond/branch_41_fun/ppermute | solution.py:243

commit v2 on v1

--- a/solution.py
+++ b/solution.py
@@ -1,3 +1,4 @@
+import functools
 import math
 
 import jax
@@ -65,68 +66,90 @@
     return re * cos + im * sin, im * cos - re * sin
 
 
-def gather_kernel(own_ref, far_ref, out_ref, local_sem, send_sem, recv_sem):
+def exchange_kernel(
+    high, partner_ref, samples_ref, out_ref, rows_ref, own_ref, pair_ref, far_ref, local_sem, pair_send, pair_recv, send_sem, recv_sem
+):
     stn = lax.axis_index("stn")
     me = lax.axis_index("tm")
     barrier = pltpu.get_barrier_semaphore()
-    for d in range(1, LINE):
-        peer = lax.rem(me + d, LINE)
-        pl.semaphore_signal(barrier, inc=1, device_id=(stn, peer), device_id_type=pl.DeviceIdType.MESH)
+    others = [(stn ^ (2 * high + low), me) for low in range(2) if 2 * high + low]
+    line = [(stn, lax.rem(me + d, LINE)) for d in range(1, LINE)]
+    for device in others + line:
+        pl.semaphore_signal(barrier, inc=1, device_id=device, device_id_type=pl.DeviceIdType.MESH)
+    for k in range(N1_BLOCK):
+        piece = samples_ref[:, k * LANES : (k + 1) * LANES].astype(F32)
+        for s in range(STN_DEV):
+            rows_ref[s, k : k + 1, :] = piece[s : s + 1, :]
+    own_ref[...] = rows_ref[...].astype(BF16)
     my_rows = pl.ds(pl.multiple_of(me * N1_BLOCK, N1_BLOCK), N1_BLOCK)
-    local = [
-        pltpu.make_async_copy(own_ref.at[pl.ds(me // 2, 1)], out_ref.at[pl.ds(0, 1), my_rows], local_sem.at[0]),
-        pltpu.make_async_copy(
-            far_ref.at[pl.ds(lax.rem(me, 2) * 2, 2)], out_ref.at[pl.ds(1, 2), my_rows], local_sem.at[1]
-        ),
-    ]
-    for copy in local:
+    pl.semaphore_wait(barrier, len(others + line))
+
+    def remote(src, dst, send, recv, device):
+        copy = pltpu.make_async_remote_copy(
+            src_ref=src, dst_ref=dst, send_sem=send, recv_sem=recv, device_id=device, device_id_type=pl.DeviceIdType.MESH
+        )
         copy.start()
+        return copy
+
+    swaps = []
+    for i, device in enumerate(others, 2 - len(others)):
+        swaps.append(remote(own_ref, pair_ref.at[i], pair_send.at[i], pair_recv.at[i], device))
+    copies = []
+    for d, device in enumerate(line, 1):
+        copies.append(
+            remote(
+                own_ref.at[pl.ds(device[1] // 2, 1)], out_ref.at[pl.ds(0, 1), my_rows], send_sem.at[0, d], recv_sem.at[0, d], device
+            )
+        )
+    local = [pltpu.make_async_copy(own_ref.at[pl.ds(me // 2, 1)], out_ref.at[pl.ds(0, 1), my_rows], local_sem.at[0])]
+    local[0].start()
     out_ref[:, WINDOWS * N1_BLOCK :, :] = jnp.zeros((3, N1_BLOCK, LANES), BF16)
-    pl.semaphore_wait(barrier, LINE - 1)
-    copies = []
-    for d in range(1, LINE):
-        peer = lax.rem(me + d, LINE)
-        for kind in (1, 0):
-            if kind:
-                src = far_ref.at[pl.ds(lax.rem(peer, 2) * 2, 2)]
-                dst = out_ref.at[pl.ds(1, 2), my_rows]
-            else:
-                src = own_ref.at[pl.ds(peer // 2, 1)]
-                dst = out_ref.at[pl.ds(0, 1), my_rows]
-            copy = pltpu.make_async_remote_copy(
-                src_ref=src,
-                dst_ref=dst,
-                send_sem=send_sem.at[kind, d],
-                recv_sem=recv_sem.at[kind, d],
-                device_id=(stn, peer),
-                device_id_type=pl.DeviceIdType.MESH,
+    for copy in swaps:
+        copy.wait()
+    far_ref[...] = pair_ref[jnp.bitwise_and(partner_ref[0], 1)] if high else pair_ref[1]
+    for d, device in enumerate(line, 1):
+        copies.append(
+            remote(
+                far_ref.at[pl.ds(lax.rem(device[1], 2) * 2, 2)],
+                out_ref.at[pl.ds(1, 2), my_rows],
+                send_sem.at[1, d],
+                recv_sem.at[1, d],
+                device,
             )
-            copy.start()
-            copies.append(copy)
-    for copy in local:
+        )
+    local.append(
+        pltpu.make_async_copy(far_ref.at[pl.ds(lax.rem(me, 2) * 2, 2)], out_ref.at[pl.ds(1, 2), my_rows], local_sem.at[1])
+    )
+    local[1].start()
+    for copy in local + copies:
         copy.wait()
-    for copy in copies:
-        copy.wait()
-
-
-def gather_line(own, far):
+
+
+def exchange(high, samples, partner):
+    block = (STN_DEV, N1_BLOCK, LANES)
     return pl.pallas_call(
-        gather_kernel,
-        name="gather_line",
+        functools.partial(exchange_kernel, high),
+        name="exchange",
         out_shape=jax.ShapeDtypeStruct((3, REC_ROWS, LANES), BF16),
-        in_specs=[pl.BlockSpec(memory_space=pltpu.VMEM)] * 2,
+        in_specs=[pl.BlockSpec(memory_space=pltpu.SMEM), pl.BlockSpec(memory_space=pltpu.VMEM)],
         out_specs=pl.BlockSpec(memory_space=pltpu.VMEM),
         scratch_shapes=[
+            pltpu.VMEM(block, F32),
+            pltpu.VMEM(block, BF16),
+            pltpu.VMEM((2,) + block, BF16),
+            pltpu.VMEM(block, BF16),
+            pltpu.SemaphoreType.DMA((2,)),
+            pltpu.SemaphoreType.DMA((2,)),
             pltpu.SemaphoreType.DMA((2,)),
             pltpu.SemaphoreType.DMA((2, LINE)),
             pltpu.SemaphoreType.DMA((2, LINE)),
         ],
-        compiler_params=pltpu.CompilerParams(collective_id=0, has_side_effects=True),
-    )(own, far)
+        compiler_params=pltpu.CompilerParams(collective_id=high, has_side_effects=True),
+    )(partner, samples)
 
 
 def correlate_kernel(
-    sizes_ref, partner_ref, place_ref, rec_ref, first_ref, twist_ref, second_ref, last_ref, share_ref,
+    sizes_ref, partner_ref, rec_ref, first_ref, twist_ref, second_ref, last_ref, share_ref,
     plain_ref, refined_ref, left_ref, spec_ref,
 ):
     cos, sin = twist_ref[:, :LANES], twist_ref[:, LANES:]
@@ -205,8 +228,8 @@
     col_hi, col_lo = halves(columns)
     lags = jnp.dot(last_ref[...], jnp.concatenate([col_hi, col_hi, col_lo], axis=0), preferred_element_type=F32)
 
-    block = place_ref[0]
-    line = place_ref[1]
+    block = lax.axis_index("stn")
+    line = lax.axis_index("tm")
     source_live = (line // 2 < sizes_ref[block]).astype(F32)
     other_size = sizes_ref[partner_ref[block]]
     for b in range(2):
@@ -218,7 +241,7 @@
                 ref[b : b + 1, k * LANES : (k + 1) * LANES] = value[k : k + 1, :]
 
 
-def correlate(array_sizes, partner, place, record):
+def correlate(array_sizes, partner, record):
     out = jax.ShapeDtypeStruct((2, LAGS), F32)
     smem = pl.BlockSpec(memory_space=pltpu.SMEM)
     vmem = pl.BlockSpec(memory_space=pltpu.VMEM)
@@ -226,26 +249,19 @@
         correlate_kernel,
         name="correlate",
         out_shape=(out, out),
-        in_specs=[smem] * 3 + [vmem] * 6,
+        in_specs=[smem] * 2 + [vmem] * 6,
         out_specs=(vmem, vmem),
         scratch_shapes=[
             pltpu.VMEM((3 * WINDOWS * ROWS, 4 * LANES), BF16),
             pltpu.VMEM((3 * WINDOWS * ROWS, 2 * LANES), F32),
         ],
-    )(array_sizes, partner, place, record, *(jnp.asarray(table) for table in tables()))
+    )(array_sizes, partner, record, *(jnp.asarray(table) for table in tables()))
 
 
 def per_device(samples, array_sizes, partner):
-    count = lax.axis_size("stn")
-    own = samples.reshape(STN_DEV, N1_BLOCK, LANES)
-
-    def moved(round_number):
-        return lambda rows: lax.ppermute(rows, "stn", [(i, i ^ round_number) for i in range(count)])
-
-    far = lax.switch(partner[0] - 1, [moved(r) for r in range(1, count)], own)
-    record = gather_line(own, far)
-    place = jnp.stack([lax.axis_index("stn"), lax.axis_index("tm")]).astype(jnp.int32)
-    return correlate(array_sizes, partner, place, record)
+    branches = [functools.partial(exchange, high) for high in range(lax.axis_size("stn") // 2)]
+    record = lax.switch(lax.shift_right_logical(partner[0], 1), branches, samples, partner)
+    return correlate(array_sizes, partner, record)
 
 
 def solution(mesh):

time: 60.1 us -> 22.7 us (0.38)
  starting transfers between devices: 19.5 us -> 0 us
  waiting for transfers between devices: 13.2 us -> 0 us
  Pallas kernels: 24.3 us -> 21 us
  local copies, waits for them, and re-layouts: 1.42 us -> 0.65 us
    ppermute x1 -> x0, starting transfers between devices: 19.5 us -> none  [moved(): lax.ppermute(rows, 'stn', [(i, i ^ round_number) for i in range(count)])]
    ppermute x1 -> x0, waiting for transfers between devices: 13.2 us -> none  [moved(): lax.ppermute(rows, 'stn', [(i, i ^ round_number) for i in range(count)])]
    pallas_call x1, Pallas kernels: 21.1 us -> 17.9 us  [exchange(): pl.pallas_call(functools.partial(exchange_kernel, high), name='exchange',...]
    unnamed x3 -> x2, local copies, waits for them, and re-layouts: 1.42 us -> 0.65 us
  transfers between devices with their start and end apart: 1 -> 0, of which waited for: 1 -> 0; matrix products, arithmetic and copies ran while one was open for 0% -> 0% of each run, Pallas kernels for 0% -> 0%
where the time goes in v2:
time: 22.7 us; the launch traced here: 22.5 us
  Pallas kernels  21 us (93%)
  between operations  0.69 us (3%)
  local copies, waits for them, and re-layouts  0.65 us (3%)
    pallas_call x1, Pallas kernels, exchange(): pl.pallas_call(functools.partial(exchange_kernel, high), name='exchange',...  17.9 us
    pallas_call x1, Pallas kernels, correlate(): pl.pallas_call(correlate_kernel, name='correlate', out_shape=(out, out),...  3.18 us
    unnamed x2, local copies, waits for them, and re-layouts  0.65 us

profile of v2, /device:TPU:1, one launch (start us, length us, event | category | flops | bytes accessed | tf_op | source)
XLA Modules:
  0.0 22.5 jit_solution(14651270594379437410)
XLA Ops:
  0.6 0.0 copy-start
  0.6 0.6 %copy-done = s32[64]{0:T(128)S(1)} copy-done((s32[64]{0:T(128)S(1)}, s32[64]{0:T(128)}, u32[]{:S(2)}) %copy-start) | copy-done | bytes 280
  1.3 17.9 %conditional.1 = (bf16[3,288,128]{2,1,0:T(8,128)(2,1)S(1)}) conditional(s32[]{:T(128)} %bitcast, (s32[64]{0:T(128)S(1)}, bf16[4,4096]{1,0:T(4,128)(2,1)}) %tuple.151, (s32[64]{0:T(128)S(1)}, bf16[4,4096]{1,0:T(4,128)(2,1)}) %tuple.167, (s32[64]{0:T(128)S(1)}, bf16[4,4096]{1,0:T(4,128)(2,1)}) %tuple.138, ...), branch_computations={%region_0.0_spmd, %region_1.0_spmd, %region_2.0_spmd, %region_3.0_... | conditional | bytes 8 | solution.py:263
  1.4 17.9 %exchange.48 = bf16[3,288,128]{2,1,0:T(8,128)(2,1)S(1)} custom-call(s32[64]{0:T(128)S(1)} %get-tuple-element.193.partner_ref, bf16[4,4096]{1,0:T(4,128)(2,1)} %get-tuple-element.194.samples_ref), custom_call_target="tpu_custom_call" | custom-call | tf_op jit(solution)/shard_map/cond/branch_16_fun/exchange/pallas_call | solution.py:130
  19.3 3.2 %correlate.1 = (f32[2,4096]{1,0:T(2,128)}, f32[2,4096]{1,0:T(2,128)}) custom-call(s32[64]{0:T(128)} %sizes_ref.1, s32[64]{0:T(128)S(1)} %copy-done, bf16[3,288,128]{2,1,0:T(8,128)(2,1)S(1)} %get-tuple-element.227.rec_ref, bf16[80,128]{1,0:T(8,128)(2,1)} %constant.19.clone.first_ref, f32[40,256]{1,0:T(8,128)} %constant.20.clone.twist_ref, ...), custom_call_target="tpu_custom_call" | custom-call | tf_op jit(solution)/shard_map/correlate/pallas_call | solution.py:248
Async XLA Ops:
  0.6 0.7 %copy-start = (s32[64]{0:T(128)S(1)}, s32[64]{0:T(128)}, u32[]{:S(2)}) copy-start(s32[64]{0:T(128)} %partner_ref.1) | copy-start | bytes 772

commit v3 on v2

--- a/solution.py
+++ b/solution.py
@@ -66,86 +66,115 @@
     return re * cos + im * sin, im * cos - re * sin
 
 
-def exchange_kernel(
-    high, partner_ref, samples_ref, out_ref, rows_ref, own_ref, pair_ref, far_ref, local_sem, pair_send, pair_recv, send_sem, recv_sem
-):
+def remote(src, dst, send, recv, device):
+    return pltpu.make_async_remote_copy(
+        src_ref=src, dst_ref=dst, send_sem=send, recv_sem=recv, device_id=device, device_id_type=pl.DeviceIdType.MESH
+    )
+
+
+def signal(semaphore, device):
+    pl.semaphore_signal(semaphore, inc=1, device_id=device, device_id_type=pl.DeviceIdType.MESH)
+
+
+def exchange_kernel(high, n_tables, partner_ref, samples_ref, *refs):
+    tables_in, out_ref, tables_out = refs[:n_tables], refs[n_tables], refs[n_tables + 1 : 2 * n_tables + 1]
+    (
+        partner_smem, samples_vmem, rows_ref, own_ref, pair_ref, in_sem, table_sem, pair_send, pair_recv, own_send, own_recv, far_send,
+        far_recv,
+    ) = refs[2 * n_tables + 1 :]
     stn = lax.axis_index("stn")
     me = lax.axis_index("tm")
+    chip, core = me // 2, lax.rem(me, 2)
     barrier = pltpu.get_barrier_semaphore()
-    others = [(stn ^ (2 * high + low), me) for low in range(2) if 2 * high + low]
-    line = [(stn, lax.rem(me + d, LINE)) for d in range(1, LINE)]
-    for device in others + line:
-        pl.semaphore_signal(barrier, inc=1, device_id=device, device_id_type=pl.DeviceIdType.MESH)
+    lows = range(0 if high else 1, 2)
+    others = [(low, to, (stn ^ (2 * high + low), 2 * chip + to)) for low in lows for to in range(2)]
+    line = [lax.rem(me + d, LINE) for d in range(1, LINE)]
+    for device in [device for _, _, device in others] + [(stn, peer) for peer in line]:
+        signal(barrier, device)
+    loads = [
+        pltpu.make_async_copy(samples_ref, samples_vmem, in_sem.at[0]),
+        pltpu.make_async_copy(partner_ref, partner_smem, in_sem.at[1]),
+    ]
+    fetches = [pltpu.make_async_copy(a, b, table_sem.at[i]) for i, (a, b) in enumerate(zip(tables_in, tables_out))]
+    for copy in loads + fetches:
+        copy.start()
+    loads[0].wait()
     for k in range(N1_BLOCK):
-        piece = samples_ref[:, k * LANES : (k + 1) * LANES].astype(F32)
+        piece = samples_vmem[:, k * LANES : (k + 1) * LANES].astype(F32)
         for s in range(STN_DEV):
             rows_ref[s, k : k + 1, :] = piece[s : s + 1, :]
     own_ref[...] = rows_ref[...].astype(BF16)
+    pl.semaphore_wait(barrier, len(others) + len(line))
+
     my_rows = pl.ds(pl.multiple_of(me * N1_BLOCK, N1_BLOCK), N1_BLOCK)
-    pl.semaphore_wait(barrier, len(others + line))
-
-    def remote(src, dst, send, recv, device):
-        copy = pltpu.make_async_remote_copy(
-            src_ref=src, dst_ref=dst, send_sem=send, recv_sem=recv, device_id=device, device_id_type=pl.DeviceIdType.MESH
+    chip_rows = pl.ds(pl.multiple_of(chip * 2 * N1_BLOCK, 2 * N1_BLOCK), 2 * N1_BLOCK)
+    core_rows = pl.ds(pl.multiple_of(core * N1_BLOCK, N1_BLOCK), N1_BLOCK)
+    swaps = [
+        remote(own_ref.at[pl.ds(2 * to, 2)], pair_ref.at[low, :, core_rows], pair_send.at[low, to], pair_recv.at[low, core], device)
+        for low, to, device in others
+    ]
+    arrivals = [
+        remote(own_ref.at[pl.ds(0, 2)], pair_ref.at[low, :, pl.ds(to * N1_BLOCK, N1_BLOCK)], pair_send.at[low, to], pair_recv.at[low, to], device)
+        for low, to, device in others
+    ]
+    for copy in swaps:
+        copy.start()
+    copies = []
+    for d, peer in enumerate(line):
+        copy = remote(
+            own_ref.at[pl.ds(peer // 2, 1)], out_ref.at[pl.ds(0, 1), my_rows], own_send.at[d], own_recv.at[d], (stn, peer)
         )
         copy.start()
-        return copy
-
-    swaps = []
-    for i, device in enumerate(others, 2 - len(others)):
-        swaps.append(remote(own_ref, pair_ref.at[i], pair_send.at[i], pair_recv.at[i], device))
-    copies = []
-    for d, device in enumerate(line, 1):
-        copies.append(
-            remote(
-                own_ref.at[pl.ds(device[1] // 2, 1)], out_ref.at[pl.ds(0, 1), my_rows], send_sem.at[0, d], recv_sem.at[0, d], device
-            )
+        copies.append(copy)
+    out_ref[0, my_rows, :] = own_ref[chip]
+    out_ref[:, WINDOWS * N1_BLOCK :, :] = jnp.zeros((3, N1_BLOCK, LANES), BF16)
+    loads[1].wait()
+    for copy in arrivals:
+        copy.wait_recv()
+    out_ref[1:3, chip_rows, :] = pair_ref[jnp.bitwise_and(partner_smem[0], 1)] if high else pair_ref[1]
+    for d in range(LINE // 2 - 1):
+        peer = lax.rem(me + 2 * (d + 1), LINE)
+        copy = remote(
+            out_ref.at[pl.ds(1, 2), chip_rows], out_ref.at[pl.ds(1, 2), chip_rows], far_send.at[d], far_recv.at[d], (stn, peer)
         )
-    local = [pltpu.make_async_copy(own_ref.at[pl.ds(me // 2, 1)], out_ref.at[pl.ds(0, 1), my_rows], local_sem.at[0])]
-    local[0].start()
-    out_ref[:, WINDOWS * N1_BLOCK :, :] = jnp.zeros((3, N1_BLOCK, LANES), BF16)
-    for copy in swaps:
+        copy.start()
+        copies.append(copy)
+    for copy in copies:
+        copy.wait_recv()
+    for copy in copies + swaps:
+        copy.wait_send()
+    for copy in fetches:
         copy.wait()
-    far_ref[...] = pair_ref[jnp.bitwise_and(partner_ref[0], 1)] if high else pair_ref[1]
-    for d, device in enumerate(line, 1):
-        copies.append(
-            remote(
-                far_ref.at[pl.ds(lax.rem(device[1], 2) * 2, 2)],
-                out_ref.at[pl.ds(1, 2), my_rows],
-                send_sem.at[1, d],
-                recv_sem.at[1, d],
-                device,
-            )
-        )
-    local.append(
-        pltpu.make_async_copy(far_ref.at[pl.ds(lax.rem(me, 2) * 2, 2)], out_ref.at[pl.ds(1, 2), my_rows], local_sem.at[1])
-    )
-    local[1].start()
-    for copy in local + copies:
-        copy.wait()
-
-
-def exchange(high, samples, partner):
+
+
+def exchange(high, samples, partner, *consts):
     block = (STN_DEV, N1_BLOCK, LANES)
+    anywhere = pl.BlockSpec(memory_space=pl.ANY)
+    vmem = pl.BlockSpec(memory_space=pltpu.VMEM)
     return pl.pallas_call(
-        functools.partial(exchange_kernel, high),
+        functools.partial(exchange_kernel, high, len(consts)),
         name="exchange",
-        out_shape=jax.ShapeDtypeStruct((3, REC_ROWS, LANES), BF16),
-        in_specs=[pl.BlockSpec(memory_space=pltpu.SMEM), pl.BlockSpec(memory_space=pltpu.VMEM)],
-        out_specs=pl.BlockSpec(memory_space=pltpu.VMEM),
+        out_shape=(jax.ShapeDtypeStruct((3, REC_ROWS, LANES), BF16),)
+        + tuple(jax.ShapeDtypeStruct(c.shape, c.dtype) for c in consts),
+        in_specs=[anywhere] * (2 + len(consts)),
+        out_specs=(vmem,) * (1 + len(consts)),
         scratch_shapes=[
+            pltpu.SMEM(partner.shape, jnp.int32),
+            pltpu.VMEM(samples.shape, BF16),
             pltpu.VMEM(block, F32),
             pltpu.VMEM(block, BF16),
-            pltpu.VMEM((2,) + block, BF16),
-            pltpu.VMEM(block, BF16),
+            pltpu.VMEM((2, 2, 2 * N1_BLOCK, LANES), BF16),
             pltpu.SemaphoreType.DMA((2,)),
-            pltpu.SemaphoreType.DMA((2,)),
-            pltpu.SemaphoreType.DMA((2,)),
-            pltpu.SemaphoreType.DMA((2, LINE)),
-            pltpu.SemaphoreType.DMA((2, LINE)),
+            pltpu.SemaphoreType.DMA((len(consts),)),
+            pltpu.SemaphoreType.DMA((2, 2)),
+            pltpu.SemaphoreType.DMA((2, 2)),
+            pltpu.SemaphoreType.DMA((LINE - 1,)),
+            pltpu.SemaphoreType.DMA((LINE - 1,)),
+            pltpu.SemaphoreType.DMA((LINE // 2 - 1,)),
+            pltpu.SemaphoreType.DMA((LINE // 2 - 1,)),
         ],
         compiler_params=pltpu.CompilerParams(collective_id=high, has_side_effects=True),
-    )(partner, samples)
+    )(partner, samples, *consts)
 
 
 def correlate_kernel(
@@ -241,7 +270,7 @@
                 ref[b : b + 1, k * LANES : (k + 1) * LANES] = value[k : k + 1, :]
 
 
-def correlate(array_sizes, partner, record):
+def correlate(array_sizes, partner, record, *consts):
     out = jax.ShapeDtypeStruct((2, LAGS), F32)
     smem = pl.BlockSpec(memory_space=pltpu.SMEM)
     vmem = pl.BlockSpec(memory_space=pltpu.VMEM)
@@ -255,13 +284,14 @@
             pltpu.VMEM((3 * WINDOWS * ROWS, 4 * LANES), BF16),
             pltpu.VMEM((3 * WINDOWS * ROWS, 2 * LANES), F32),
         ],
-    )(array_sizes, partner, record, *(jnp.asarray(table) for table in tables()))
+    )(array_sizes, partner, record, *consts)
 
 
 def per_device(samples, array_sizes, partner):
     branches = [functools.partial(exchange, high) for high in range(lax.axis_size("stn") // 2)]
-    record = lax.switch(lax.shift_right_logical(partner[0], 1), branches, samples, partner)
-    return correlate(array_sizes, partner, record)
+    consts = [jnp.asarray(table) for table in tables()]
+    staged = lax.switch(lax.shift_right_logical(partner[0], 1), branches, samples, partner, *consts)
+    return correlate(array_sizes, partner, *staged)
 
 
 def solution(mesh):

time: 22.7 us -> 26.7 us (1.18)
  Pallas kernels: 21 us -> 25.2 us
    pallas_call x1, Pallas kernels: 17.9 us -> 22.3 us  [exchange(): pl.pallas_call(functools.partial(exchange_kernel, high, len(consts)), nam...]
    pallas_call x1, Pallas kernels: 3.18 us -> 2.85 us  [correlate(): pl.pallas_call(correlate_kernel, name='correlate', out_shape=(out, out),...]
where the time goes in v3:
time: 26.7 us; the launch traced here: 26.6 us
  Pallas kernels  25.2 us (94%)
  between operations  0.69 us (3%)
  local copies, waits for them, and re-layouts  0.65 us (2%)
    pallas_call x1, Pallas kernels, exchange(): pl.pallas_call(functools.partial(exchange_kernel, high, len(consts)), nam...  22.3 us
    pallas_call x1, Pallas kernels, correlate(): pl.pallas_call(correlate_kernel, name='correlate', out_shape=(out, out),...  2.85 us
    unnamed x2, local copies, waits for them, and re-layouts  0.65 us

profile of v3, /device:TPU:1, one launch (start us, length us, event | category | flops | bytes accessed | tf_op | source)
XLA Modules:
  0.0 26.6 jit_solution(911767661530408927)
XLA Ops:
  0.6 0.0 copy-start
  0.6 0.6 %copy-done = s32[64]{0:T(128)S(1)} copy-done((s32[64]{0:T(128)S(1)}, s32[64]{0:T(128)}, u32[]{:S(2)}) %copy-start) | copy-done | bytes 280
  1.3 22.4 %conditional.1 = ((bf16[3,288,128]{2,1,0:T(8,128)(2,1)S(1)}, bf16[80,128]{1,0:T(8,128)(2,1)S(1)}, f32[40,256]{1,0:T(8,128)S(1)}, bf16[256,512]{1,0:T(8,128)(2,1)...) conditional(s32[]{:T(128)} %bitcast, (s32[64]{0:T(128)S(1)}, ...), branch_computations={%region_0.0_spmd, %region_1.0_spmd, %region_2.0_spmd, %region_3.0_... | conditional | bytes 8 | solution.py:293
  1.4 22.3 %exchange.44 = (bf16[3,288,128]{2,1,0:T(8,128)(2,1)S(1)}, bf16[80,128]{1,0:T(8,128)(2,1)S(1)}, f32[40,256]{1,0:T(8,128)S(1)}, bf16[256,512]{1,0:T(8,128)(2,1)S(1...) custom-call(s32[64]{0:T(128)S(1)} %get-tuple-element.532.partner_ref, ...), custom_call_target="tpu_custom_call" | custom-call | tf_op jit(solution)/shard_map/cond/branch_12_fun/exchange/pallas_call | solution.py:154
  23.7 2.8 %correlate.1 = (f32[2,4096]{1,0:T(2,128)}, f32[2,4096]{1,0:T(2,128)}) custom-call(s32[64]{0:T(128)} %sizes_ref.1, s32[64]{0:T(128)S(1)} %copy-done, bf16[3,288,128]{2,1,0:T(8,128)(2,1)S(1)} %get-tuple-element.680.rec_ref, bf16[80,128]{1,0:T(8,128)(2,1)S(1)} %get-tuple-element.681.first_ref, f32[40,256]{1,0:T(8,128)S(1)} %get-tuple-element.682.twist_ref, ...), custom_call_target="tpu_custom_call" | custom-call | tf_op jit(solution)/shard_map/correlate/pallas_call | solution.py:277
Async XLA Ops:
  0.6 0.7 %copy-start = (s32[64]{0:T(128)S(1)}, s32[64]{0:T(128)}, u32[]{:S(2)}) copy-start(s32[64]{0:T(128)} %partner_ref.1) | copy-start | bytes 772

commit v4 on v3

--- a/solution.py
+++ b/solution.py
@@ -20,6 +20,7 @@
 HALO = 2
 ROWS = 40
 N1_BLOCK = LAGS // LANES
+HALF = N1_BLOCK // 2
 REC_ROWS = (WINDOWS + 1) * N1_BLOCK
 SMALL = 1e-06
 F32 = jnp.float32
@@ -79,17 +80,22 @@
 def exchange_kernel(high, n_tables, partner_ref, samples_ref, *refs):
     tables_in, out_ref, tables_out = refs[:n_tables], refs[n_tables], refs[n_tables + 1 : 2 * n_tables + 1]
     (
-        partner_smem, samples_vmem, rows_ref, own_ref, pair_ref, in_sem, table_sem, pair_send, pair_recv, own_send, own_recv, far_send,
+        partner_smem, samples_vmem, rows_ref, own_ref, pair_ref, pick_ref, land_ref, in_sem, table_sem, pair_send, pair_recv, own_send, own_recv, far_send,
         far_recv,
     ) = refs[2 * n_tables + 1 :]
     stn = lax.axis_index("stn")
     me = lax.axis_index("tm")
     chip, core = me // 2, lax.rem(me, 2)
     barrier = pltpu.get_barrier_semaphore()
-    lows = range(0 if high else 1, 2)
-    others = [(low, to, (stn ^ (2 * high + low), 2 * chip + to)) for low in lows for to in range(2)]
+    others = [(low, to, (stn ^ (2 * high + low), 2 * chip + to)) for low in range(2) for to in range(2)]
+    if not high:
+        others = others[2:]
     line = [lax.rem(me + d, LINE) for d in range(1, LINE)]
-    for device in [device for _, _, device in others] + [(stn, peer) for peer in line]:
+    column = [lax.rem(me + 2 * d, LINE) for d in range(LINE // 2)]
+    mate = me + 1 - 2 * core
+    near = [device for _, _, device in others] + [(stn, peer) for peer in line]
+    near += [(stn ^ 1, peer) for peer in (column if high else column[1:])]
+    for device in near:
         signal(barrier, device)
     loads = [
         pltpu.make_async_copy(samples_ref, samples_vmem, in_sem.at[0]),
@@ -99,24 +105,35 @@
     for copy in loads + fetches:
         copy.start()
     loads[0].wait()
-    for k in range(N1_BLOCK):
-        piece = samples_vmem[:, k * LANES : (k + 1) * LANES].astype(F32)
+
+    @pl.loop(0, N1_BLOCK)
+    def _(k):
+        piece = samples_vmem[:, pl.ds(pl.multiple_of(k * LANES, LANES), LANES)].astype(F32)
         for s in range(STN_DEV):
-            rows_ref[s, k : k + 1, :] = piece[s : s + 1, :]
+            rows_ref[s, pl.ds(k, 1), :] = piece[s : s + 1, :]
+
     own_ref[...] = rows_ref[...].astype(BF16)
-    pl.semaphore_wait(barrier, len(others) + len(line))
+    pl.semaphore_wait(barrier, len(near))
 
     my_rows = pl.ds(pl.multiple_of(me * N1_BLOCK, N1_BLOCK), N1_BLOCK)
-    chip_rows = pl.ds(pl.multiple_of(chip * 2 * N1_BLOCK, 2 * N1_BLOCK), 2 * N1_BLOCK)
-    core_rows = pl.ds(pl.multiple_of(core * N1_BLOCK, N1_BLOCK), N1_BLOCK)
     swaps = [
-        remote(own_ref.at[pl.ds(2 * to, 2)], pair_ref.at[low, :, core_rows], pair_send.at[low, to], pair_recv.at[low, core], device)
+        remote(
+            own_ref.at[pl.ds(2 * to, 2), pl.ds(low * HALF, HALF)], pair_ref.at[low, core], pair_send.at[low, to], pair_recv.at[low, core],
+            device,
+        )
         for low, to, device in others
     ]
     arrivals = [
-        remote(own_ref.at[pl.ds(0, 2)], pair_ref.at[low, :, pl.ds(to * N1_BLOCK, N1_BLOCK)], pair_send.at[low, to], pair_recv.at[low, to], device)
+        remote(own_ref.at[pl.ds(0, 2), pl.ds(0, HALF)], pair_ref.at[low, to], pair_send.at[low, to], pair_recv.at[low, to], device)
         for low, to, device in others
     ]
+    if not high:
+        kept = remote(
+            own_ref.at[pl.ds(2 - 2 * core, 2), pl.ds(0, HALF)], pair_ref.at[0, core], pair_send.at[0, 0], pair_recv.at[0, 0], (stn, mate)
+        )
+        swaps.append(kept)
+        arrivals.append(kept)
+        pair_ref[0, core] = own_ref[pl.ds(2 * core, 2), :HALF]
     for copy in swaps:
         copy.start()
     copies = []
@@ -131,16 +148,24 @@
     loads[1].wait()
     for copy in arrivals:
         copy.wait_recv()
-    out_ref[1:3, chip_rows, :] = pair_ref[jnp.bitwise_and(partner_smem[0], 1)] if high else pair_ref[1]
-    for d in range(LINE // 2 - 1):
-        peer = lax.rem(me + 2 * (d + 1), LINE)
-        copy = remote(
-            out_ref.at[pl.ds(1, 2), chip_rows], out_ref.at[pl.ds(1, 2), chip_rows], far_send.at[d], far_recv.at[d], (stn, peer)
-        )
-        copy.start()
-        copies.append(copy)
+    bit = jnp.bitwise_and(partner_smem[0], 1)
+    pick_ref[0] = pair_ref[bit]
+    pick_ref[1] = pair_ref[1 - bit]
+    for cross in range(2):
+        for d in range(1 - cross, LINE // 2):
+            copy = remote(
+                pick_ref.at[cross], land_ref.at[cross, chip], far_send.at[cross, d], far_recv.at[cross, d], (stn ^ cross, column[d])
+            )
+            copy.start()
+            copies.append(copy)
+    land_ref[0, chip] = pick_ref[0]
     for copy in copies:
         copy.wait_recv()
+    for half in range(2):
+        blocks = land_ref[bit if half == 0 else 1 - bit]
+        for sender in range(LINE):
+            start = sender * N1_BLOCK + half * HALF
+            out_ref[1:3, start : start + HALF, :] = blocks[sender // 2, sender % 2]
     for copy in copies + swaps:
         copy.wait_send()
     for copy in fetches:
@@ -149,6 +174,7 @@
 
 def exchange(high, samples, partner, *consts):
     block = (STN_DEV, N1_BLOCK, LANES)
+    half = (2, 2, HALF, LANES)
     anywhere = pl.BlockSpec(memory_space=pl.ANY)
     vmem = pl.BlockSpec(memory_space=pltpu.VMEM)
     return pl.pallas_call(
@@ -163,15 +189,17 @@
             pltpu.VMEM(samples.shape, BF16),
             pltpu.VMEM(block, F32),
             pltpu.VMEM(block, BF16),
-            pltpu.VMEM((2, 2, 2 * N1_BLOCK, LANES), BF16),
+            pltpu.VMEM((2,) + half, BF16),
+            pltpu.VMEM((2,) + half, BF16),
+            pltpu.VMEM((2, LINE // 2) + half, BF16),
             pltpu.SemaphoreType.DMA((2,)),
             pltpu.SemaphoreType.DMA((len(consts),)),
             pltpu.SemaphoreType.DMA((2, 2)),
             pltpu.SemaphoreType.DMA((2, 2)),
             pltpu.SemaphoreType.DMA((LINE - 1,)),
             pltpu.SemaphoreType.DMA((LINE - 1,)),
-            pltpu.SemaphoreType.DMA((LINE // 2 - 1,)),
-            pltpu.SemaphoreType.DMA((LINE // 2 - 1,)),
+            pltpu.SemaphoreType.DMA((2, LINE // 2)),
+            pltpu.SemaphoreType.DMA((2, LINE // 2)),
         ],
         compiler_params=pltpu.CompilerParams(collective_id=high, has_side_effects=True),
     )(partner, samples, *consts)
@@ -179,8 +207,14 @@
 
 def correlate_kernel(
     sizes_ref, partner_ref, rec_ref, first_ref, twist_ref, second_ref, last_ref, share_ref,
-    plain_ref, refined_ref, left_ref, spec_ref,
+    plain_ref, refined_ref, left_ref, spec_ref, sizes_smem, partner_smem, in_sem,
 ):
+    loads = [
+        pltpu.make_async_copy(sizes_ref, sizes_smem, in_sem.at[0]),
+        pltpu.make_async_copy(partner_ref, partner_smem, in_sem.at[1]),
+    ]
+    for copy in loads:
+        copy.start()
     cos, sin = twist_ref[:, :LANES], twist_ref[:, LANES:]
     cos2, sin2 = jnp.concatenate([cos, cos], axis=0), jnp.concatenate([sin, sin], axis=0)
     first = first_ref[...]
@@ -257,10 +291,12 @@
     col_hi, col_lo = halves(columns)
     lags = jnp.dot(last_ref[...], jnp.concatenate([col_hi, col_hi, col_lo], axis=0), preferred_element_type=F32)
 
+    for copy in loads:
+        copy.wait()
     block = lax.axis_index("stn")
     line = lax.axis_index("tm")
-    source_live = (line // 2 < sizes_ref[block]).astype(F32)
-    other_size = sizes_ref[partner_ref[block]]
+    source_live = (line // 2 < sizes_smem[block]).astype(F32)
+    other_size = sizes_smem[partner_smem[block]]
     for b in range(2):
         live = source_live * (lax.rem(line, 2) * 2 + b < other_size).astype(F32)
         for kind, ref in enumerate((plain_ref, refined_ref)):
@@ -272,17 +308,19 @@
 
 def correlate(array_sizes, partner, record, *consts):
     out = jax.ShapeDtypeStruct((2, LAGS), F32)
-    smem = pl.BlockSpec(memory_space=pltpu.SMEM)
     vmem = pl.BlockSpec(memory_space=pltpu.VMEM)
     return pl.pallas_call(
         correlate_kernel,
         name="correlate",
         out_shape=(out, out),
-        in_specs=[smem] * 2 + [vmem] * 6,
+        in_specs=[pl.BlockSpec(memory_space=pl.ANY)] * 2 + [vmem] * 6,
         out_specs=(vmem, vmem),
         scratch_shapes=[
             pltpu.VMEM((3 * WINDOWS * ROWS, 4 * LANES), BF16),
             pltpu.VMEM((3 * WINDOWS * ROWS, 2 * LANES), F32),
+            pltpu.SMEM(array_sizes.shape, jnp.int32),
+            pltpu.SMEM(partner.shape, jnp.int32),
+            pltpu.SemaphoreType.DMA((2,)),
         ],
     )(array_sizes, partner, record, *consts)
 

time: 26.7 us -> 23.9 us (0.90)
  Pallas kernels: 25.2 us -> 22.4 us
    pallas_call x1, Pallas kernels: 22.3 us -> 20.1 us  [exchange(): pl.pallas_call(functools.partial(exchange_kernel, high, len(consts)), nam...]
    pallas_call x1, Pallas kernels: 2.85 us -> 2.26 us  [correlate(): pl.pallas_call(correlate_kernel, name='correlate', out_shape=(out, out),...]
where the time goes in v4:
time: 23.9 us; the launch traced here: 23.8 us
  Pallas kernels  22.4 us (94%)
  between operations  0.69 us (3%)
  local copies, waits for them, and re-layouts  0.65 us (3%)
    pallas_call x1, Pallas kernels, exchange(): pl.pallas_call(functools.partial(exchange_kernel, high, len(consts)), nam...  20.1 us
    pallas_call x1, Pallas kernels, correlate(): pl.pallas_call(correlate_kernel, name='correlate', out_shape=(out, out),...  2.26 us
    unnamed x2, local copies, waits for them, and re-layouts  0.65 us

profile of v4, /device:TPU:1, one launch (start us, length us, event | category | flops | bytes accessed | tf_op | source)
XLA Modules:
  0.0 23.8 jit_solution(2340062901005256253)
XLA Ops:
  0.6 0.0 copy-start
  0.6 0.6 %copy-done = s32[64]{0:T(128)S(1)} copy-done((s32[64]{0:T(128)S(1)}, s32[64]{0:T(128)}, u32[]{:S(2)}) %copy-start) | copy-done | bytes 280
  1.3 20.2 %conditional.1 = ((bf16[3,288,128]{2,1,0:T(8,128)(2,1)S(1)}, bf16[80,128]{1,0:T(8,128)(2,1)S(1)}, f32[40,256]{1,0:T(8,128)S(1)}, bf16[256,512]{1,0:T(8,128)(2,1)...) conditional(s32[]{:T(128)} %bitcast, (s32[64]{0:T(128)S(1)}, ...), branch_computations={%region_0.0_spmd, %region_1.0_spmd, %region_2.0_spmd, %region_3.0_... | conditional | bytes 8 | solution.py:331
  1.4 20.1 %exchange.42 = (bf16[3,288,128]{2,1,0:T(8,128)(2,1)S(1)}, bf16[80,128]{1,0:T(8,128)(2,1)S(1)}, f32[40,256]{1,0:T(8,128)S(1)}, bf16[256,512]{1,0:T(8,128)(2,1)S(1...) custom-call(s32[64]{0:T(128)S(1)} %get-tuple-element.518.partner_ref, ...), custom_call_target="tpu_custom_call" | custom-call | tf_op jit(solution)/shard_map/cond/branch_10_fun/exchange/pallas_call | solution.py:180
  21.5 2.3 %correlate.1 = (f32[2,4096]{1,0:T(2,128)}, f32[2,4096]{1,0:T(2,128)}) custom-call(s32[64]{0:T(128)} %sizes_ref.1, s32[64]{0:T(128)S(1)} %copy-done, bf16[3,288,128]{2,1,0:T(8,128)(2,1)S(1)} %get-tuple-element.680.rec_ref, bf16[80,128]{1,0:T(8,128)(2,1)S(1)} %get-tuple-element.681.first_ref, f32[40,256]{1,0:T(8,128)S(1)} %get-tuple-element.682.twist_ref, ...), custom_call_target="tpu_custom_call" | custom-call | tf_op jit(solution)/shard_map/correlate/pallas_call | solution.py:312
Async XLA Ops:
  0.6 0.7 %copy-start = (s32[64]{0:T(128)S(1)}, s32[64]{0:T(128)}, u32[]{:S(2)}) copy-start(s32[64]{0:T(128)} %partner_ref.1) | copy-start | bytes 772

commit v5 on v4

--- a/solution.py
+++ b/solution.py
@@ -88,13 +88,10 @@
     chip, core = me // 2, lax.rem(me, 2)
     barrier = pltpu.get_barrier_semaphore()
     others = [(low, to, (stn ^ (2 * high + low), 2 * chip + to)) for low in range(2) for to in range(2)]
-    if not high:
-        others = others[2:]
     line = [lax.rem(me + d, LINE) for d in range(1, LINE)]
     column = [lax.rem(me + 2 * d, LINE) for d in range(LINE // 2)]
-    mate = me + 1 - 2 * core
     near = [device for _, _, device in others] + [(stn, peer) for peer in line]
-    near += [(stn ^ 1, peer) for peer in (column if high else column[1:])]
+    near += [(stn ^ 1, peer) for peer in column]
     for device in near:
         signal(barrier, device)
     loads = [
@@ -106,7 +103,7 @@
         copy.start()
     loads[0].wait()
 
-    @pl.loop(0, N1_BLOCK)
+    @pl.loop(0, N1_BLOCK, unroll=4)
     def _(k):
         piece = samples_vmem[:, pl.ds(pl.multiple_of(k * LANES, LANES), LANES)].astype(F32)
         for s in range(STN_DEV):
@@ -127,13 +124,6 @@
         remote(own_ref.at[pl.ds(0, 2), pl.ds(0, HALF)], pair_ref.at[low, to], pair_send.at[low, to], pair_recv.at[low, to], device)
         for low, to, device in others
     ]
-    if not high:
-        kept = remote(
-            own_ref.at[pl.ds(2 - 2 * core, 2), pl.ds(0, HALF)], pair_ref.at[0, core], pair_send.at[0, 0], pair_recv.at[0, 0], (stn, mate)
-        )
-        swaps.append(kept)
-        arrivals.append(kept)
-        pair_ref[0, core] = own_ref[pl.ds(2 * core, 2), :HALF]
     for copy in swaps:
         copy.start()
     copies = []
@@ -151,7 +141,7 @@
     bit = jnp.bitwise_and(partner_smem[0], 1)
     pick_ref[0] = pair_ref[bit]
     pick_ref[1] = pair_ref[1 - bit]
-    for cross in range(2):
+    for cross in (1, 0):
         for d in range(1 - cross, LINE // 2):
             copy = remote(
                 pick_ref.at[cross], land_ref.at[cross, chip], far_send.at[cross, d], far_recv.at[cross, d], (stn ^ cross, column[d])
@@ -200,6 +190,110 @@
             pltpu.SemaphoreType.DMA((LINE - 1,)),
             pltpu.SemaphoreType.DMA((2, LINE // 2)),
             pltpu.SemaphoreType.DMA((2, LINE // 2)),
+        ],
+        compiler_params=pltpu.CompilerParams(collective_id=high, has_side_effects=True),
+    )(partner, samples, *consts)
+
+
+def direct_kernel(high, n_tables, partner_ref, samples_ref, *refs):
+    tables_in, out_ref, tables_out = refs[:n_tables], refs[n_tables], refs[n_tables + 1 : 2 * n_tables + 1]
+    (
+        partner_smem, samples_vmem, rows_ref, own_ref, pair_ref, in_sem, table_sem, pair_send, pair_recv, own_send, own_recv, far_send,
+        far_recv,
+    ) = refs[2 * n_tables + 1 :]
+    stn = lax.axis_index("stn")
+    me = lax.axis_index("tm")
+    chip, core = me // 2, lax.rem(me, 2)
+    barrier = pltpu.get_barrier_semaphore()
+    lows = range(0 if high else 1, 2)
+    others = [(low, to, (stn ^ (2 * high + low), 2 * chip + to)) for low in lows for to in range(2)]
+    line = [lax.rem(me + d, LINE) for d in range(1, LINE)]
+    for device in [device for _, _, device in others] + [(stn, peer) for peer in line]:
+        signal(barrier, device)
+    loads = [
+        pltpu.make_async_copy(samples_ref, samples_vmem, in_sem.at[0]),
+        pltpu.make_async_copy(partner_ref, partner_smem, in_sem.at[1]),
+    ]
+    fetches = [pltpu.make_async_copy(a, b, table_sem.at[i]) for i, (a, b) in enumerate(zip(tables_in, tables_out))]
+    for copy in loads + fetches:
+        copy.start()
+    loads[0].wait()
+
+    @pl.loop(0, N1_BLOCK, unroll=4)
+    def _(k):
+        piece = samples_vmem[:, pl.ds(pl.multiple_of(k * LANES, LANES), LANES)].astype(F32)
+        for s in range(STN_DEV):
+            rows_ref[s, pl.ds(k, 1), :] = piece[s : s + 1, :]
+
+    own_ref[...] = rows_ref[...].astype(BF16)
+    pl.semaphore_wait(barrier, len(others) + len(line))
+
+    my_rows = pl.ds(pl.multiple_of(me * N1_BLOCK, N1_BLOCK), N1_BLOCK)
+    chip_rows = pl.ds(pl.multiple_of(chip * 2 * N1_BLOCK, 2 * N1_BLOCK), 2 * N1_BLOCK)
+    core_rows = pl.ds(pl.multiple_of(core * N1_BLOCK, N1_BLOCK), N1_BLOCK)
+    swaps = [
+        remote(own_ref.at[pl.ds(2 * to, 2)], pair_ref.at[low, :, core_rows], pair_send.at[low, to], pair_recv.at[low, core], device)
+        for low, to, device in others
+    ]
+    arrivals = [
+        remote(own_ref.at[pl.ds(0, 2)], pair_ref.at[low, :, pl.ds(to * N1_BLOCK, N1_BLOCK)], pair_send.at[low, to], pair_recv.at[low, to], device)
+        for low, to, device in others
+    ]
+    for copy in swaps:
+        copy.start()
+    copies = []
+    for d, peer in enumerate(line):
+        copy = remote(
+            own_ref.at[pl.ds(peer // 2, 1)], out_ref.at[pl.ds(0, 1), my_rows], own_send.at[d], own_recv.at[d], (stn, peer)
+        )
+        copy.start()
+        copies.append(copy)
+    out_ref[0, my_rows, :] = own_ref[chip]
+    out_ref[:, WINDOWS * N1_BLOCK :, :] = jnp.zeros((3, N1_BLOCK, LANES), BF16)
+    loads[1].wait()
+    for copy in arrivals:
+        copy.wait_recv()
+    out_ref[1:3, chip_rows, :] = pair_ref[jnp.bitwise_and(partner_smem[0], 1)] if high else pair_ref[1]
+    for d in range(LINE // 2 - 1):
+        peer = lax.rem(me + 2 * (d + 1), LINE)
+        copy = remote(
+            out_ref.at[pl.ds(1, 2), chip_rows], out_ref.at[pl.ds(1, 2), chip_rows], far_send.at[d], far_recv.at[d], (stn, peer)
+        )
+        copy.start()
+        copies.append(copy)
+    for copy in copies:
+        copy.wait_recv()
+    for copy in copies + swaps:
+        copy.wait_send()
+    for copy in fetches:
+        copy.wait()
+
+
+def exchange_direct(high, samples, partner, *consts):
+    block = (STN_DEV, N1_BLOCK, LANES)
+    anywhere = pl.BlockSpec(memory_space=pl.ANY)
+    vmem = pl.BlockSpec(memory_space=pltpu.VMEM)
+    return pl.pallas_call(
+        functools.partial(direct_kernel, high, len(consts)),
+        name="exchange_direct",
+        out_shape=(jax.ShapeDtypeStruct((3, REC_ROWS, LANES), BF16),)
+        + tuple(jax.ShapeDtypeStruct(c.shape, c.dtype) for c in consts),
+        in_specs=[anywhere] * (2 + len(consts)),
+        out_specs=(vmem,) * (1 + len(consts)),
+        scratch_shapes=[
+            pltpu.SMEM(partner.shape, jnp.int32),
+            pltpu.VMEM(samples.shape, BF16),
+            pltpu.VMEM(block, F32),
+            pltpu.VMEM(block, BF16),
+            pltpu.VMEM((2, 2, 2 * N1_BLOCK, LANES), BF16),
+            pltpu.SemaphoreType.DMA((2,)),
+            pltpu.SemaphoreType.DMA((len(consts),)),
+            pltpu.SemaphoreType.DMA((2, 2)),
+            pltpu.SemaphoreType.DMA((2, 2)),
+            pltpu.SemaphoreType.DMA((LINE - 1,)),
+            pltpu.SemaphoreType.DMA((LINE - 1,)),
+            pltpu.SemaphoreType.DMA((LINE // 2 - 1,)),
+            pltpu.SemaphoreType.DMA((LINE // 2 - 1,)),
         ],
         compiler_params=pltpu.CompilerParams(collective_id=high, has_side_effects=True),
     )(partner, samples, *consts)
@@ -326,7 +420,8 @@
 
 
 def per_device(samples, array_sizes, partner):
-    branches = [functools.partial(exchange, high) for high in range(lax.axis_size("stn") // 2)]
+    near = [high % 8 == 0 for high in range(lax.axis_size("stn") // 2)]
+    branches = [functools.partial(exchange_direct if n else exchange, high) for high, n in enumerate(near)]
     consts = [jnp.asarray(table) for table in tables()]
     staged = lax.switch(lax.shift_right_logical(partner[0], 1), branches, samples, partner, *consts)
     return correlate(array_sizes, partner, *staged)

time: 23.9 us -> 19.2 us (0.80)
  Pallas kernels: 22.4 us -> 17.6 us
    pallas_call x1, Pallas kernels: 20.1 us -> 15.3 us  [exchange_direct(): pl.pallas_call(functools.partial(direct_kernel, high, len(consts)), name=...]
where the time goes in v5:
time: 19.2 us; the launch traced here: 19 us
  Pallas kernels  17.6 us (92%)
  between operations  0.69 us (4%)
  local copies, waits for them, and re-layouts  0.65 us (3%)
    pallas_call x1, Pallas kernels, exchange_direct(): pl.pallas_call(functools.partial(direct_kernel, high, len(consts)), name=...  15.3 us
    pallas_call x1, Pallas kernels, correlate(): pl.pallas_call(correlate_kernel, name='correlate', out_shape=(out, out),...  2.26 us
    unnamed x2, local copies, waits for them, and re-layouts  0.65 us

profile of v5, /device:TPU:1, one launch (start us, length us, event | category | flops | bytes accessed | tf_op | source)
XLA Modules:
  0.0 19.0 jit_solution(1329959675053302486)
XLA Ops:
  0.6 0.0 copy-start
  0.6 0.6 %copy-done = s32[64]{0:T(128)S(1)} copy-done((s32[64]{0:T(128)S(1)}, s32[64]{0:T(128)}, u32[]{:S(2)}) %copy-start) | copy-done | bytes 280
  1.3 15.4 %conditional.1 = ((bf16[3,288,128]{2,1,0:T(8,128)(2,1)S(1)}, bf16[80,128]{1,0:T(8,128)(2,1)S(1)}, f32[40,256]{1,0:T(8,128)S(1)}, bf16[256,512]{1,0:T(8,128)(2,1)...) conditional(s32[]{:T(128)} %bitcast, (s32[64]{0:T(128)S(1)}, ...), branch_computations={%region_0.0_spmd, %region_1.0_spmd, %region_2.0_spmd, %region_3.0_... | conditional | bytes 8 | solution.py:426
  1.4 15.3 %exchange_direct.5 = (bf16[3,288,128]{2,1,0:T(8,128)(2,1)S(1)}, bf16[80,128]{1,0:T(8,128)(2,1)S(1)}, f32[40,256]{1,0:T(8,128)S(1)}, bf16[256,512]{1,0:T(8,128)(2...) custom-call(s32[64]{0:T(128)S(1)} %get-tuple-element.504.partner_ref, ...), custom_call_target="tpu_custom_call" | custom-call | tf_op jit(solution)/shard_map/cond/branch_8_fun/exchange_direct/pallas_call | solution.py:276
  16.7 2.3 %correlate.1 = (f32[2,4096]{1,0:T(2,128)}, f32[2,4096]{1,0:T(2,128)}) custom-call(s32[64]{0:T(128)} %sizes_ref.1, s32[64]{0:T(128)S(1)} %copy-done, bf16[3,288,128]{2,1,0:T(8,128)(2,1)S(1)} %get-tuple-element.680.rec_ref, bf16[80,128]{1,0:T(8,128)(2,1)S(1)} %get-tuple-element.681.first_ref, f32[40,256]{1,0:T(8,128)S(1)} %get-tuple-element.682.twist_ref, ...), custom_call_target="tpu_custom_call" | custom-call | tf_op jit(solution)/shard_map/correlate/pallas_call | solution.py:406
Async XLA Ops:
  0.6 0.7 %copy-start = (s32[64]{0:T(128)S(1)}, s32[64]{0:T(128)}, u32[]{:S(2)}) copy-start(s32[64]{0:T(128)} %partner_ref.1) | copy-start | bytes 772
